TPU v7x, 256 devices: a whole 4x4x8 slice. The times are simulated.
256 devices in a mesh: slab: 64 (over y, z, x_lo), ffn: 4 (over x_hi, core).
Axes of the slice: x: 4 (x_hi: 2, x_lo: 2; x = x_hi * 2 + x_lo), y: 4, z: 8, core: 2. Of those that a mesh axis runs over, the one named last changes fastest.
Arguments:
- tokens: bfloat16 [32768, 512], P('slab'), may hold values from -6 to 6
- gain_attn: float32 [512], replicated, may hold values from 0.1 to 1.9
- w_reduce: bfloat16 [4096, 512], replicated, may hold values from -0.09375 to 0.09375
- gain_keys: float32 [512], replicated, may hold values from 0.1 to 1.9
- w_query: bfloat16 [512, 512], P(None, 'ffn'), may hold values from -1.5 to 1.5
- w_key: bfloat16 [512, 512], P(None, 'ffn'), may hold values from -1.5 to 1.5
- w_value: bfloat16 [512, 512], P(None, 'ffn'), may hold values from -0.25 to 0.25
- w_out: bfloat16 [512, 512], P('ffn'), may hold values from -1.796875 to 1.796875
- gain_ffn: float32 [512], replicated, may hold values from 0.1 to 1.9
- w_up: bfloat16 [512, 2048], P(None, 'ffn'), may hold values from -0.25 to 0.25
- w_depth: float32 [27, 2048], P(None, 'ffn'), may hold values from -1.25 to 1.25
- w_down: bfloat16 [2048, 512], P('ffn'), may hold values from -0.125 to 0.125
- grad_out: bfloat16 [32768, 512], P('slab'), may hold values from -0.0625 to 0.0625
Outputs:
- attended: bfloat16 [32768, 512], P('slab')
- grad_up: float32 [512, 2048], P('slab', 'ffn')
- grad_down: float32 [512, 2048], P('slab', 'ffn')
All inputs are finite; a program needn't handle non-finite values.
Results may differ from a plain program's by a relative error of at most 0.024.
The roundings to bfloat16 on the way count: a program that leaves them out, or rounds other values in their place, can miss the bound.
Values may be sent and summed in bfloat16 or wider, within the bound.
A program may use at most 64 MiB of HBM per device.

v0:
```python
import math
import jax
import jax.numpy as jnp
from jax import lax
from jax.sharding import PartitionSpec as P

HEAD = 64
GX = 16
GY = 16
CZ = 2
EPSILON = 1e-05
ROPE_BASE = 100.0
ROOT_HALF = 0.7071067811865476
NORMAL_SCALE = 0.3989422804014327


def padded_2(cells, sides, width):
    for axis, dim in sides:
        count = lax.axis_size(axis)
        ends = count - 1
        head = lax.slice_in_dim(cells, 0, width, axis=dim)
        tail = lax.slice_in_dim(cells, cells.shape[dim] - width, cells.shape[dim], axis=dim)
        cells = jnp.concatenate(
            [
                lax.ppermute(tail, axis, [(i, (i + 1) % count) for i in range(ends)]),
                cells,
                lax.ppermute(head, axis, [((i + 1) % count, i) for i in range(ends)]),
            ],
            axis=dim,
        )
    return cells


def layer_norm(values, scale_gain):
    values = values.astype(jnp.float32)
    centered = values - jnp.mean(values, axis=-1, keepdims=True)
    variance = jnp.mean(centered * centered, axis=-1, keepdims=True)
    return centered * lax.rsqrt(variance + EPSILON) * scale_gain


def rope_tables(coord_x, coord_y, coord_z, head_size):
    pair_count = head_size // 2
    position = jnp.arange(pair_count, dtype=jnp.int32)
    axis_pick = position % 3
    per_axis = (pair_count + 2) // 3
    frequency = ROPE_BASE ** (-(position // 3).astype(jnp.float32) / per_axis)
    angles = (
        coord_x[:, None] * (axis_pick == 0)
        + coord_y[:, None] * (axis_pick == 1)
        + coord_z[:, None] * (axis_pick == 2)
    ) * frequency
    return (jnp.cos(angles)[:, None, :], jnp.sin(angles)[:, None, :])


def token_tables(first_plane, planes, head_size):
    position = jnp.arange(planes * GY * GX, dtype=jnp.int32)
    coord_x = (position % GX).astype(jnp.float32)
    coord_y = (position // GX % GY).astype(jnp.float32)
    coord_z = (first_plane + position // (GX * GY)).astype(jnp.float32)
    return rope_tables(coord_x, coord_y, coord_z, head_size)


def key_tables(first_row, row_count, head_size):
    position = first_row + jnp.arange(row_count, dtype=jnp.int32)
    half_x = GX // 2
    half_y = GY // 2
    coord_x = (position % half_x).astype(jnp.float32) * 2.0 + 0.5
    coord_y = (position // half_x % half_y).astype(jnp.float32) * 2.0 + 0.5
    coord_z = (position // (half_x * half_y)).astype(jnp.float32) * 2.0 + 0.5
    return rope_tables(coord_x, coord_y, coord_z, head_size)


def rotate(values, cosine, sine_table):
    half_size = values.shape[-1] // 2
    front_half = values[..., :half_size]
    back_half = values[..., half_size:]
    return jnp.concatenate(
        [
            front_half * cosine - back_half * sine_table,
            back_half * cosine + front_half * sine_table,
        ],
        axis=-1,
    )


def make_patches(normed, planes):
    width = normed.shape[-1]
    cell_grid = normed.reshape(planes // 2, 2, GY // 2, 2, GX // 2, 2, width)
    return cell_grid.transpose(0, 2, 4, 1, 3, 5, 6).reshape(-1, 8 * width)


def depth_conv(padded, weights, planes):
    height = padded.shape[1] - 2
    width_x = padded.shape[2] - 2
    result = jnp.zeros((planes, height, width_x, padded.shape[3]), jnp.float32)
    for offset in range(27):
        shift_z = offset // 9
        shift_y = offset // 3 % 3
        shift_x = offset % 3
        window = padded[
            shift_z : shift_z + planes, shift_y : shift_y + height, shift_x : shift_x + width_x
        ]
        result = result + window.astype(jnp.float32) * weights[offset]
    return result


def attend_piece(state_tuple, queries, key_rows, value_rows):
    row_max, row_sum, weighted = state_tuple
    score_scale = key_rows.shape[-1] ** (-0.5)
    scores = (
        jnp.einsum("qhd,khd->hqk", queries, key_rows, preferred_element_type=jnp.float32)
        * score_scale
    )
    new_max = jnp.maximum(row_max, jnp.max(scores, axis=2))
    rescale = jnp.exp(row_max - new_max)
    expo = jnp.exp(scores - new_max[:, :, None])
    row_sum = row_sum * rescale + jnp.sum(expo, axis=2)
    weighted = weighted * rescale[:, :, None] + jnp.einsum(
        "hqk,khd->hqd", expo.astype(jnp.bfloat16), value_rows, preferred_element_type=jnp.float32
    )
    return (new_max, row_sum, weighted)


def per_device(
    tokens,
    gain_attn,
    w_reduce,
    gain_keys,
    w_query,
    w_key,
    w_value,
    w_out,
    gain_ffn,
    w_up,
    w_depth,
    w_down,
    grad_out,
):
    slab_index = lax.axis_index("slab")
    tok_rows = tokens.shape[0]
    heads_dev = w_query.shape[1] // HEAD
    normed = layer_norm(tokens, gain_attn).astype(jnp.bfloat16)
    patches = make_patches(normed, CZ)
    reduced = jnp.dot(patches, w_reduce, preferred_element_type=jnp.float32)
    key_input = layer_norm(reduced, gain_keys).astype(jnp.bfloat16)
    tok_cos, tok_sin = token_tables(slab_index * CZ, CZ, HEAD)
    queries = jnp.dot(normed, w_query, preferred_element_type=jnp.float32).reshape(
        tok_rows, heads_dev, HEAD
    )
    queries = rotate(queries, tok_cos, tok_sin).astype(jnp.bfloat16)
    initial = (
        jnp.full((heads_dev, tok_rows), -1e30, jnp.float32),
        jnp.zeros((heads_dev, tok_rows), jnp.float32),
        jnp.zeros((heads_dev, tok_rows, HEAD), jnp.float32),
    )
    state_tuple = initial
    pieces = lax.all_gather(key_input, "slab", axis=0, tiled=True)
    row_count = pieces.shape[0]
    block_rows = math.gcd(row_count, 1024)
    block_count = row_count // block_rows
    blocks = pieces.reshape(block_count, block_rows, pieces.shape[1])

    def one_block(state_inner, block_item):
        rows_in, block_index = block_item
        block_first = block_index * block_rows
        key_cos, key_sin = key_tables(block_first, block_rows, HEAD)
        key_block = jnp.dot(rows_in, w_key, preferred_element_type=jnp.float32).reshape(
            block_rows, heads_dev, HEAD
        )
        key_block = rotate(key_block, key_cos, key_sin).astype(jnp.bfloat16)
        value_block = (
            jnp.dot(rows_in, w_value, preferred_element_type=jnp.float32)
            .astype(jnp.bfloat16)
            .reshape(block_rows, heads_dev, HEAD)
        )
        return (attend_piece(state_inner, queries, key_block, value_block), None)

    state_tuple, _ = lax.scan(
        one_block, state_tuple, (blocks, jnp.arange(block_count, dtype=jnp.int32))
    )
    row_max, row_sum, weighted = state_tuple
    heads_out = (
        (weighted / row_sum[:, :, None])
        .transpose(1, 0, 2)
        .reshape(tok_rows, heads_dev * HEAD)
        .astype(jnp.bfloat16)
    )
    partial_value = jnp.dot(heads_out, w_out, preferred_element_type=jnp.float32)
    head_total = lax.psum(partial_value.astype(jnp.bfloat16), "ffn").astype(jnp.float32)
    attended = head_total.astype(jnp.bfloat16)
    residual = tokens.astype(jnp.float32) + head_total
    normed_ffn = layer_norm(residual, gain_ffn).astype(jnp.bfloat16)
    channels = w_up.shape[1]
    pre = (
        jnp.dot(normed_ffn, w_up, preferred_element_type=jnp.float32)
        .astype(jnp.bfloat16)
        .reshape(CZ, GY, GX, channels)
    )
    pre_wide = padded_2(pre, (("slab", 0),), 1)
    pre_pad = jnp.pad(pre_wide, ((0, 0), (1, 1), (1, 1), (0, 0)))
    mixed = depth_conv(pre_pad, w_depth, CZ).reshape(tok_rows, channels)
    normal_cdf = 0.5 * (1.0 + lax.erf(mixed * ROOT_HALF))
    normal_pdf = jnp.exp(-0.5 * mixed * mixed) * NORMAL_SCALE
    activated = (mixed * normal_cdf).astype(jnp.bfloat16)
    grad_act = jnp.einsum("td,cd->tc", grad_out, w_down, preferred_element_type=jnp.float32)
    grad_mixed = (
        (grad_act * (normal_cdf + mixed * normal_pdf))
        .astype(jnp.bfloat16)
        .reshape(CZ, GY, GX, channels)
    )
    grad_wide = padded_2(grad_mixed, (("slab", 0),), 1)
    grad_pad = jnp.pad(grad_wide, ((0, 0), (1, 1), (1, 1), (0, 0)))
    grad_pre = (
        depth_conv(grad_pad, w_depth[::-1], CZ).astype(jnp.bfloat16).reshape(tok_rows, channels)
    )
    up_full = jnp.einsum("td,tc->dc", normed_ffn, grad_pre, preferred_element_type=jnp.float32)
    down_full = jnp.einsum("td,tc->dc", grad_out, activated, preferred_element_type=jnp.float32)
    grads = lax.psum_scatter(
        jnp.concatenate([up_full, down_full], axis=1), "slab", scatter_dimension=0, tiled=True
    )
    return (attended, grads[:, :channels], grads[:, channels:])


def solution(mesh):
    in_specs = (
        P("slab", None),
        P(),
        P(),
        P(),
        P(None, "ffn"),
        P(None, "ffn"),
        P(None, "ffn"),
        P("ffn", None),
        P(),
        P(None, "ffn"),
        P(None, "ffn"),
        P("ffn", None),
        P("slab", None),
    )
    out_specs = (P("slab", None), P("slab", "ffn"), P("slab", "ffn"))
    return jax.shard_map(
        per_device, mesh=mesh, in_specs=in_specs, out_specs=out_specs, check_vma=False
    )
```

profile of v0, /device:TPU:4, one launch (start us, length us, event | category | flops | bytes accessed | tf_op | source)
XLA Modules:
  0.0 795.7 jit_solution(1866074170113802012)
XLA Ops:
  12.2 3.2 fusion.96
  17.3 306.8 %all-gather.2.cloned.1.call-done = bf16[4096,512]{1,0:T(8,128)(2,1)} async-done(((bf16[64,512]{1,0:T(8,128)(2,1)}), bf16[4096,512]{1,0:T(8,128)(2,1)}) %all-gather.2.cloned.1.call-update) | async-done | bytes 4194320 | tf_op jit(solution)/shard_map/all_gather | solution.py:157
  324.1 48.4 %while.18 = (s32[]{:T(128)}, f32[2,512]{1,0:T(2,128)S(1)}, f32[2,512]{1,0:T(2,128)S(1)}, f32[2,512,64]{1,2,0:T(8,128)S(1)}, bf16[4,1024,512]{2,1,0:T(8,128)(2,1)...) while((s32[]{:T(128)}, f32[2,512]{1,0:T(2,128)S(1)}, ...), condition=%wide.region_7.8_spmd.clone, body=%wide.region_4.7_spmd.clone.sunk | while | flops 546895744 | bytes 35088572 | solution.py:178
  326.0 1.7 fusion.137
  327.8 2.7 bitcast_reduce_fusion.2
  330.5 3.0 fusion.143
  333.6 1.7 convolution_convert_fusion.4
  338.1 1.7 fusion.137
  339.9 2.7 bitcast_reduce_fusion.2
  342.6 3.0 fusion.143
  345.7 1.7 convolution_convert_fusion.4
  350.2 1.7 fusion.137
  352.0 2.7 bitcast_reduce_fusion.2
  354.7 3.0 fusion.143
  357.8 1.7 convolution_convert_fusion.4
  362.3 1.7 fusion.137
  364.1 2.7 bitcast_reduce_fusion.2
  366.9 3.0 fusion.143
  369.9 1.7 convolution_convert_fusion.4
  373.8 41.8 %all-reduce.4.cloned.1.call-done = bf16[512,512]{1,0:T(8,128)(2,1)} async-done(((bf16[512,512]{1,0:T(8,128)(2,1)}), bf16[512,512]{1,0:T(8,128)(2,1)}) %all-reduce.4.cloned.1.call-update) | async-done | bytes 524304 | tf_op jit(solution)/shard_map/psum | solution.py:189
  418.2 1.6 convolution_convert_fusion.1
  419.9 3.7 collective-permute-start
  425.0 10.3 %collective-permute-done = bf16[1,16,16,512]{3,2,1,0:T(8,128)(2,1)S(1)} collective-permute-done((bf16[1,16,16,512]{3,2,1,0:T(8,128)(2,1)S(1)}, bf16[1,16,16,512]{3,2,1,0:T(8,128)(2,1)S(1)}, u32[]{:S(2)}, u32[]{:S(2)}) %collective-permute-start) | collective-permute-done | bytes 262176 | tf_op jit(solution)/shard_map/ppermute | solution.py:25
  435.2 3.5 collective-permute-done.1
  439.5 3.8 multiply_add_fusion
  444.2 1.5 collective-permute-start.2
  445.7 1.5 collective-permute-start.3
  447.7 9.5 %collective-permute-done.2 = bf16[1,16,16,512]{3,2,1,0:T(8,128)(2,1)S(1)} collective-permute-done((bf16[1,16,16,512]{3,2,1,0:T(8,128)(2,1)S(1)}, bf16[1,16,16,512]{3,2,1,0:T(8,128)(2,1)S(1)}, u32[]{:S(2)}, u32[]{:S(2)}) %collective-permute-start.2) | collective-permute-done | bytes 262176 | tf_op jit(solution)/shard_map/ppermute | solution.py:25
  457.2 4.1 collective-permute-done.3
  462.1 3.8 add_convert_fusion.1
  466.8 1.8 copy.31
  468.7 318.3 %reduce-scatter.4.cloned.1.call-done = f32[8,1024]{1,0:T(8,128)} async-done(((f32[512,1024]{1,0:T(8,128)}), f32[8,1024]{1,0:T(8,128)}) %reduce-scatter.4.cloned.1.call-update) | async-done | bytes 32784
  (134 shorter events, 26.5 us)
Async XLA Ops:
  7.2 436.4 %copy-start = (bf16[512,512]{1,0:T(8,128)(2,1)S(1)}, bf16[512,512]{1,0:T(8,128)(2,1)}, u32[]{:S(2)}) copy-start(bf16[512,512]{1,0:T(8,128)(2,1)} %param.27) | copy-start | bytes 1572868
  7.2 316.9 %all-gather.2.cloned.1.call-start = ((), (), s32[]{:S(2)}) async-start(), calls=%async_computation.1 | async-start | bytes 4259840 | tf_op jit(solution)/shard_map/all_gather | solution.py:157
  11.3 4.2 copy-start.11
  11.3 5.1 copy-start.8
  11.7 5.2 copy-start.7
  12.1 311.9 %copy-start.5 = (bf16[512,128]{1,0:T(8,128)(2,1)S(1)}, bf16[512,128]{1,0:T(8,128)(2,1)}, u32[]{:S(2)}) copy-start(bf16[512,128]{1,0:T(8,128)(2,1)} %param.21) | copy-start | bytes 393220
  16.3 399.3 %all-reduce.4.cloned.1.call-start = ((), (), s32[]{:S(2)}) async-start(), calls=%async_computation.2 | async-start | bytes 1048576 | tf_op jit(solution)/shard_map/psum | solution.py:189
  324.1 48.5 %copy-start.9 = (bf16[128,512]{1,0:T(8,128)(2,1)S(1)}, bf16[128,512]{1,0:T(8,128)(2,1)}, u32[]{:S(2)}) copy-start(bf16[128,512]{1,0:T(8,128)(2,1)} %param.22) | copy-start | bytes 393220
  324.1 91.5 %copy-start.2 = (bf16[512,512]{1,0:T(8,128)(2,1)S(1)}, bf16[512,512]{1,0:T(8,128)(2,1)}, u32[]{:S(2)}) copy-start(bf16[512,512]{1,0:T(8,128)(2,1)} %param.15) | copy-start | bytes 1572868
  330.5 4.8 copy-start.1
  342.6 4.8 copy-start.1
  354.7 4.8 copy-start.1
  366.8 4.8 copy-start.1
  372.5 45.7 %copy-start.12 = (bf16[512,512]{1,0:T(8,128)(2,1)S(1)}, bf16[512,512]{1,0:T(8,128)(2,1)}, u32[]{:S(2)}) copy-start(bf16[512,512]{1,0:T(8,128)(2,1)} %param.24) | copy-start | bytes 1572868
  372.5 45.7 %copy-start.13 = (f32[512]{0:T(512)S(1)}, f32[512]{0:T(512)}, u32[]{:S(2)}) copy-start(f32[512]{0:T(512)} %param.23) | copy-start | bytes 6148
  372.6 52.3 %copy-start.10 = (f32[27,512]{1,0:T(8,128)S(1)}, f32[27,512]{1,0:T(8,128)}, u32[]{:S(2)}) copy-start(f32[27,512]{1,0:T(8,128)} %param.25) | copy-start | bytes 165892
  373.8 413.3 %reduce-scatter.4.cloned.1.call-start = ((), (), s32[]{:S(2)}) async-start(), calls=%async_computation.3 | async-start | bytes 2129920
  419.9 15.4 %collective-permute-start = (bf16[1,16,16,512]{3,2,1,0:T(8,128)(2,1)S(1)}, bf16[1,16,16,512]{3,2,1,0:T(8,128)(2,1)S(1)}, u32[]{:S(2)}, u32[]{:S(2)}) collective-permute-start(bf16[1,16,16,512]{3,2,1,0:T(8,128)(2,1)S(1)} %bitcast.133), channel_id=1, source_target_pairs={{0,4},{4,8},{8,12},{12,16},{16,20},{20,24},{24,28},{28,32},{32,36}... | collective-permute-start | bytes 786440 | tf_op jit(solution)/shard_map/ppermute | solution.py:25
  423.6 15.2 %collective-permute-start.1 = (bf16[1,16,16,512]{3,2,1,0:T(8,128)(2,1)S(1)}, bf16[1,16,16,512]{3,2,1,0:T(8,128)(2,1)S(1)}, u32[]{:S(2)}, u32[]{:S(2)}) collective-permute-start(bf16[1,16,16,512]{3,2,1,0:T(8,128)(2,1)S(1)} %bitcast.132), channel_id=1, source_target_pairs={{4,0},{8,4},{12,8},{16,12},{20,16},{24,20},{28,24},{32,28},{36,32}... | collective-permute-start | bytes 786440 | tf_op jit(solution)/shard_map/ppermute | solution.py:27
  439.5 4.1 copy-start.6
  444.2 12.9 %collective-permute-start.2 = (bf16[1,16,16,512]{3,2,1,0:T(8,128)(2,1)S(1)}, bf16[1,16,16,512]{3,2,1,0:T(8,128)(2,1)S(1)}, u32[]{:S(2)}, u32[]{:S(2)}) collective-permute-start(bf16[1,16,16,512]{3,2,1,0:T(8,128)(2,1)S(1)} %bitcast.135), channel_id=1, source_target_pairs={{0,4},{4,8},{8,12},{12,16},{16,20},{20,24},{24,28},{28,32},{32,36}... | collective-permute-start | bytes 786440 | tf_op jit(solution)/shard_map/ppermute | solution.py:25
  445.7 15.6 %collective-permute-start.3 = (bf16[1,16,16,512]{3,2,1,0:T(8,128)(2,1)S(1)}, bf16[1,16,16,512]{3,2,1,0:T(8,128)(2,1)S(1)}, u32[]{:S(2)}, u32[]{:S(2)}) collective-permute-start(bf16[1,16,16,512]{3,2,1,0:T(8,128)(2,1)S(1)} %bitcast.134), channel_id=1, source_target_pairs={{4,0},{8,4},{12,8},{16,12},{20,16},{24,20},{28,24},{32,28},{36,32}... | collective-permute-start | bytes 786440 | tf_op jit(solution)/shard_map/ppermute | solution.py:27
  462.1 3.9 copy-start.3
  466.8 321.6 %copy-start.4 = (bf16[512,512]{1,0:T(8,128)(2,1)S(1)}, bf16[512,512]{1,0:T(8,128)(2,1)}, u32[]{:S(2)}) copy-start(bf16[512,512]{1,0:T(8,128)(2,1)} %all-reduce.4.cloned.1.call-done) | copy-start | bytes 1572868
Sparse Core Ops, SparseCore 0:
  16.4 307.6 all-gather.1
  373.9 41.6 all-reduce.3
  468.8 318.1 reduce-scatter.3
where the time goes:
time: 796 us
  waiting for transfers between devices  694 us (87%)
  matrix products  35.8 us (4%)
  other arithmetic  32.5 us (4%)
  between operations  14.2 us (2%)
  starting transfers between devices  8.07 us (1%)
    unnamed x4, waiting for transfers between devices  318 us
    all_gather x1, waiting for transfers between devices, per_device(): pieces = lax.all_gather(key_input, 'slab', axis=0, tiled=True)  307 us
    psum x1, waiting for transfers between devices, per_device(): lax.psum(partial_value.astype(jnp.bfloat16), 'ffn').astype(jnp.float32)  41.8 us
    ppermute x2, waiting for transfers between devices, padded_2(): lax.ppermute(tail, axis, [(i, (i + 1) % count) for i in range(ends)])  19.8 us
  transfers between devices with their start and end apart: 7, of which 7 were waited for; matrix products, arithmetic and copies ran while one was open for 0% of the time, Pallas kernels for 0%

commit v1 on v0

--- a/solution.py
+++ b/solution.py
@@ -12,6 +12,11 @@
 ROPE_BASE = 100.0
 ROOT_HALF = 0.7071067811865476
 NORMAL_SCALE = 0.3989422804014327
+
+
+def register_weights(row_data, along_axis="ffn"):
+    front = jax.lax.all_gather(row_data, axis_name=along_axis)
+    return jnp.sum(front, 0)
 
 
 def padded_2(cells, sides, width):
@@ -186,7 +191,7 @@
         .astype(jnp.bfloat16)
     )
     partial_value = jnp.dot(heads_out, w_out, preferred_element_type=jnp.float32)
-    head_total = lax.psum(partial_value.astype(jnp.bfloat16), "ffn").astype(jnp.float32)
+    head_total = register_weights(partial_value.astype(jnp.bfloat16)).astype(jnp.float32)
     attended = head_total.astype(jnp.bfloat16)
     residual = tokens.astype(jnp.float32) + head_total
     normed_ffn = layer_norm(residual, gain_ffn).astype(jnp.bfloat16)

time: 796 us -> 776 us (0.975)
  waiting for transfers between devices: 694 us -> 676 us
    psum x1 -> x0, waiting for transfers between devices: 41.8 us -> none  [per_device(): lax.psum(partial_value.astype(jnp.bfloat16), 'ffn').astype(jnp.float32)]
    all_gather x0 -> x1, waiting for transfers between devices: none -> 23.3 us  [register_weights(): front = jax.lax.all_gather(row_data, axis_name=along_axis)]
where the time goes in v1:
time: 776 us
  waiting for transfers between devices  676 us (87%)
  matrix products  34.8 us (4%)
  other arithmetic  32.7 us (4%)
  between operations  14.2 us (2%)
  starting transfers between devices  8.58 us (1%)
    unnamed x4, waiting for transfers between devices  318 us
    all_gather x1, waiting for transfers between devices, per_device(): pieces = lax.all_gather(key_input, 'slab', axis=0, tiled=True)  307 us
    all_gather x1, waiting for transfers between devices, register_weights(): front = jax.lax.all_gather(row_data, axis_name=along_axis)  23.3 us
    ppermute x2, waiting for transfers between devices, padded_2(): lax.ppermute(tail, axis, [(i, (i + 1) % count) for i in range(ends)])  19.7 us
  transfers between devices with their start and end apart: 7, of which 7 were waited for; matrix products, arithmetic and copies ran while one was open for 0% of the time, Pallas kernels for 0%

profile of v1, /device:TPU:4, one launch (start us, length us, event | category | flops | bytes accessed | tf_op | source)
XLA Modules:
  0.0 775.8 jit_solution(14083238668236426655)
XLA Ops:
  12.2 3.2 fusion.96
  17.3 306.8 %all-gather.4.cloned.1.call-done = bf16[4096,512]{1,0:T(8,128)(2,1)} async-done(((bf16[64,512]{1,0:T(8,128)(2,1)}), bf16[4096,512]{1,0:T(8,128)(2,1)}) %all-gather.4.cloned.1.call-update) | async-done | bytes 4194320 | tf_op jit(solution)/shard_map/all_gather | solution.py:162
  324.1 48.4 %while.18 = (s32[]{:T(128)}, f32[2,512]{1,0:T(2,128)S(1)}, f32[2,512]{1,0:T(2,128)S(1)}, f32[2,512,64]{1,2,0:T(8,128)S(1)}, bf16[4,1024,512]{2,1,0:T(8,128)(2,1)...) while((s32[]{:T(128)}, f32[2,512]{1,0:T(2,128)S(1)}, ...), condition=%wide.region_7.8_spmd.clone, body=%wide.region_4.7_spmd.clone.sunk | while | flops 546895744 | bytes 35088572 | solution.py:183
  326.0 1.7 fusion.137
  327.8 2.7 bitcast_reduce_fusion.2
  330.5 3.0 fusion.143
  333.6 1.7 convolution_convert_fusion.4
  338.1 1.7 fusion.137
  339.9 2.7 bitcast_reduce_fusion.2
  342.6 3.0 fusion.143
  345.7 1.7 convolution_convert_fusion.4
  350.2 1.7 fusion.137
  352.0 2.7 bitcast_reduce_fusion.2
  354.7 3.0 fusion.143
  357.8 1.7 convolution_convert_fusion.4
  362.3 1.7 fusion.137
  364.1 2.7 bitcast_reduce_fusion.2
  366.8 3.0 fusion.143
  369.9 1.7 convolution_convert_fusion.4
  373.8 23.3 %all-gather.6.cloned.1.call-done = bf16[2048,512]{1,0:T(8,128)(2,1)} async-done(((bf16[512,512]{1,0:T(8,128)(2,1)}), bf16[2048,512]{1,0:T(8,128)(2,1)}) %all-gather.6.cloned.1.call-update) | async-done | bytes 2097168 | tf_op jit(solution)/shard_map/all_gather | solution.py:18
  397.1 2.2 reduce_sum.83
  400.5 4.2 collective-permute-start
  406.1 10.2 %collective-permute-done = bf16[1,16,16,512]{3,2,1,0:T(8,128)(2,1)S(1)} collective-permute-done((bf16[1,16,16,512]{3,2,1,0:T(8,128)(2,1)S(1)}, bf16[1,16,16,512]{3,2,1,0:T(8,128)(2,1)S(1)}, u32[]{:S(2)}, u32[]{:S(2)}) %collective-permute-start) | collective-permute-done | bytes 262176 | tf_op jit(solution)/shard_map/ppermute | solution.py:30
  416.3 3.5 collective-permute-done.1
  420.5 3.8 multiply_add_fusion
  425.2 1.5 collective-permute-start.2
  426.7 1.5 collective-permute-start.3
  428.7 9.5 %collective-permute-done.2 = bf16[1,16,16,512]{3,2,1,0:T(8,128)(2,1)S(1)} collective-permute-done((bf16[1,16,16,512]{3,2,1,0:T(8,128)(2,1)S(1)}, bf16[1,16,16,512]{3,2,1,0:T(8,128)(2,1)S(1)}, u32[]{:S(2)}, u32[]{:S(2)}) %collective-permute-start.2) | collective-permute-done | bytes 262176 | tf_op jit(solution)/shard_map/ppermute | solution.py:30
  438.2 4.1 collective-permute-done.3
  443.1 3.8 add_convert_fusion.1
  447.9 1.8 copy.31
  449.7 318.2 %reduce-scatter.4.cloned.1.call-done = f32[8,1024]{1,0:T(8,128)} async-done(((f32[512,1024]{1,0:T(8,128)}), f32[8,1024]{1,0:T(8,128)}) %reduce-scatter.4.cloned.1.call-update) | async-done | bytes 32784
  (132 shorter events, 24.3 us)
Async XLA Ops:
  7.2 417.5 %copy-start = (bf16[512,512]{1,0:T(8,128)(2,1)S(1)}, bf16[512,512]{1,0:T(8,128)(2,1)}, u32[]{:S(2)}) copy-start(bf16[512,512]{1,0:T(8,128)(2,1)} %param.27) | copy-start | bytes 1572868
  7.2 316.9 %all-gather.4.cloned.1.call-start = ((), (), s32[]{:S(2)}) async-start(), calls=%async_computation.1 | async-start | bytes 4259840 | tf_op jit(solution)/shard_map/all_gather | solution.py:162
  11.3 4.2 copy-start.10
  11.3 5.1 copy-start.7
  11.7 5.2 copy-start.6
  12.1 311.9 %copy-start.4 = (bf16[512,128]{1,0:T(8,128)(2,1)S(1)}, bf16[512,128]{1,0:T(8,128)(2,1)}, u32[]{:S(2)}) copy-start(bf16[512,128]{1,0:T(8,128)(2,1)} %param.21) | copy-start | bytes 393220
  16.3 380.8 %all-gather.6.cloned.1.call-start = ((), (), s32[]{:S(2)}) async-start(), calls=%async_computation.2 | async-start | bytes 2621440 | tf_op jit(solution)/shard_map/all_gather | solution.py:18
  324.1 48.5 %copy-start.8 = (bf16[128,512]{1,0:T(8,128)(2,1)S(1)}, bf16[128,512]{1,0:T(8,128)(2,1)}, u32[]{:S(2)}) copy-start(bf16[128,512]{1,0:T(8,128)(2,1)} %param.22) | copy-start | bytes 393220
  330.5 4.8 copy-start.1
  342.6 4.8 copy-start.1
  354.7 4.8 copy-start.1
  366.8 4.8 copy-start.1
  372.5 26.8 %copy-start.2 = (bf16[512,512]{1,0:T(8,128)(2,1)S(1)}, bf16[512,512]{1,0:T(8,128)(2,1)}, u32[]{:S(2)}) copy-start(bf16[512,512]{1,0:T(8,128)(2,1)} %param.15) | copy-start | bytes 1572868
  372.5 27.3 %copy-start.11 = (bf16[512,512]{1,0:T(8,128)(2,1)S(1)}, bf16[512,512]{1,0:T(8,128)(2,1)}, u32[]{:S(2)}) copy-start(bf16[512,512]{1,0:T(8,128)(2,1)} %param.24) | copy-start | bytes 1572868
  372.6 27.3 %copy-start.12 = (f32[512]{0:T(512)S(1)}, f32[512]{0:T(512)}, u32[]{:S(2)}) copy-start(f32[512]{0:T(512)} %param.23) | copy-start | bytes 6148
  373.8 394.2 %reduce-scatter.4.cloned.1.call-start = ((), (), s32[]{:S(2)}) async-start(), calls=%async_computation.3 | async-start | bytes 2129920
  399.3 47.6 %copy-start.3 = (bf16[512,512]{1,0:T(8,128)(2,1)}, bf16[512,512]{1,0:T(8,128)(2,1)S(1)}, u32[]{:S(2)}) copy-start(bf16[512,512]{1,0:T(8,128)(2,1)S(1)} %reduce_sum.83) | copy-start | bytes 1572868
  399.3 6.7 copy-start.9
  400.5 15.8 %collective-permute-start = (bf16[1,16,16,512]{3,2,1,0:T(8,128)(2,1)S(1)}, bf16[1,16,16,512]{3,2,1,0:T(8,128)(2,1)S(1)}, u32[]{:S(2)}, u32[]{:S(2)}) collective-permute-start(bf16[1,16,16,512]{3,2,1,0:T(8,128)(2,1)S(1)} %bitcast.135), channel_id=1, source_target_pairs={{0,4},{4,8},{8,12},{12,16},{16,20},{20,24},{24,28},{28,32},{32,36}... | collective-permute-start | bytes 786440 | tf_op jit(solution)/shard_map/ppermute | solution.py:30
  404.7 15.0 %collective-permute-start.1 = (bf16[1,16,16,512]{3,2,1,0:T(8,128)(2,1)S(1)}, bf16[1,16,16,512]{3,2,1,0:T(8,128)(2,1)S(1)}, u32[]{:S(2)}, u32[]{:S(2)}) collective-permute-start(bf16[1,16,16,512]{3,2,1,0:T(8,128)(2,1)S(1)} %bitcast.134), channel_id=1, source_target_pairs={{4,0},{8,4},{12,8},{16,12},{20,16},{24,20},{28,24},{32,28},{36,32}... | collective-permute-start | bytes 786440 | tf_op jit(solution)/shard_map/ppermute | solution.py:32
  420.5 4.1 copy-start.5
  425.2 12.9 %collective-permute-start.2 = (bf16[1,16,16,512]{3,2,1,0:T(8,128)(2,1)S(1)}, bf16[1,16,16,512]{3,2,1,0:T(8,128)(2,1)S(1)}, u32[]{:S(2)}, u32[]{:S(2)}) collective-permute-start(bf16[1,16,16,512]{3,2,1,0:T(8,128)(2,1)S(1)} %bitcast.137), channel_id=1, source_target_pairs={{0,4},{4,8},{8,12},{12,16},{16,20},{20,24},{24,28},{28,32},{32,36}... | collective-permute-start | bytes 786440 | tf_op jit(solution)/shard_map/ppermute | solution.py:30
  426.7 15.6 %collective-permute-start.3 = (bf16[1,16,16,512]{3,2,1,0:T(8,128)(2,1)S(1)}, bf16[1,16,16,512]{3,2,1,0:T(8,128)(2,1)S(1)}, u32[]{:S(2)}, u32[]{:S(2)}) collective-permute-start(bf16[1,16,16,512]{3,2,1,0:T(8,128)(2,1)S(1)} %bitcast.136), channel_id=1, source_target_pairs={{4,0},{8,4},{12,8},{16,12},{20,16},{24,20},{28,24},{32,28},{36,32}... | collective-permute-start | bytes 786440 | tf_op jit(solution)/shard_map/ppermute | solution.py:32
Sparse Core Ops, SparseCore 0:
  16.4 307.6 all-gather.3
  373.9 23.2 all-gather.5
  449.9 318.0 reduce-scatter.3
